TPU v7x, 32 devices: a whole 2x2x4 slice. The times are simulated.
32 devices in a mesh: corpus: 4 (over z), rerank: 8 (over y, x, core).
Axes of the slice: x: 2, y: 2, z: 4, core: 2. Of those that a mesh axis runs over, the one named last changes fastest.
Arguments:
- store_rows: bfloat16 [128, 512, 3584], P('corpus', 'rerank'), may hold values from -400 to 400
- block_lengths: int32 [128], replicated, may hold values from 128 to 512
- queries: bfloat16 [32, 64, 3584], P(None, 'rerank'), may hold values from -400 to 400
- cand_owner: int32 [64, 1], replicated, may hold values from 0 to 3; in each aligned block of 16 rows (0 to 15, 16 to 31, ...) at most 5 rows name the same one
- cand_block: int32 [64], replicated, may hold values from 0 to 31
- cand_query: int32 [64], replicated, may hold values from 0 to 31
- norm_gain: bfloat16 [3584], replicated, may hold values from 0.099609375 to 1.8984375
- w_query: bfloat16 [3584, 1792], P('rerank'), may hold values from -8 to 8
- w_key: bfloat16 [3584, 256], P('rerank'), may hold values from -1 to 1
- w_value: bfloat16 [3584, 256], P('rerank'), may hold values from -0.09375 to 0.09375
- w_score: bfloat16 [1792], replicated, may hold values from -0.125 to 0.125
Outputs:
- passage_context: bfloat16 [80, 512, 1792], P('corpus', 'rerank')
- pair_scores: float32 [64], P(('corpus', 'rerank'))
Inputs may be any that keep to these rules, and one draw needn't show every extreme that they name: `cand_owner`: at most 5 of the 16 pairs of one corpus group (an aligned block of rows) name the same owner, in every draw, some group names one owner in exactly 5 of its 16 pairs.
All inputs are finite; a program needn't handle non-finite values.
Results may differ from a plain program's by a relative error of at most 0.013.
Values may be sent and summed in bfloat16 or wider, within the bound.
A program may use at most 128 MiB of HBM per device.

v0:
```python
import jax
import jax.numpy as jnp
from jax import lax
from jax.sharding import PartitionSpec as P

HDIM = 128
QHEADS = 14
KVHEADS = 2
BLK = 512
CAP = 5
ROPE_BASE = 1000000.0
EPSILON = 1e-06


def rotate(values, positions):
    head_dim = values.shape[-1]
    half_dim = head_dim // 2
    inverse = jnp.power(ROPE_BASE, -2.0 * jnp.arange(half_dim, dtype=jnp.float32) / head_dim)
    angles = positions.astype(jnp.float32)[..., None] * inverse
    cosine = jnp.cos(angles)[..., None, :]
    sine_part = jnp.sin(angles)[..., None, :]
    lower = values[..., :half_dim]
    upper = values[..., half_dim:]
    return jnp.concatenate(
        [lower * cosine - upper * sine_part, upper * cosine + lower * sine_part], axis=-1
    )


def pick_rows(table, wanted, indices):
    present = jnp.any(wanted, axis=1)
    picked = jnp.sum(jnp.where(wanted, indices[None, :], 0), axis=1)
    chosen = jnp.take(table, picked, axis=0)
    return jnp.where(present[:, None, None], chosen, jnp.zeros((), table.dtype))


def add_products(pieces, columns):
    return (
        jnp.dot(columns, pieces[0], preferred_element_type=jnp.float32),
        jnp.dot(columns, pieces[1], preferred_element_type=jnp.float32),
        jnp.dot(columns, pieces[2], preferred_element_type=jnp.float32),
    )


def attend_one(items):
    query_rot, key_rot, values, length = items
    seq_len = query_rot.shape[0]
    token_ids = jnp.arange(seq_len, dtype=jnp.int32)
    grouped = query_rot.reshape(seq_len, KVHEADS, QHEADS // KVHEADS, HDIM)
    logits = jnp.einsum(
        "skgd,tkd->kgst", grouped, key_rot, preferred_element_type=jnp.float32
    ) * HDIM ** (-0.5)
    live = (token_ids < length) | (token_ids >= BLK)
    allowed = live[None, :] & (token_ids[None, :] <= token_ids[:, None])
    masked = jnp.where(allowed, logits, -1e30)
    peak = jnp.max(masked, axis=-1, keepdims=True)
    weights = jnp.where(allowed, jnp.exp(masked - peak), 0.0)
    probs = (weights / jnp.sum(weights, axis=-1, keepdims=True)).astype(jnp.bfloat16)
    context = jnp.einsum("kgst,tkd->skgd", probs, values, preferred_element_type=jnp.float32)
    return context.reshape(seq_len, QHEADS * HDIM).astype(jnp.bfloat16)


def on_device(
    store_rows,
    block_lengths,
    queries,
    cand_owner,
    cand_block,
    cand_query,
    norm_gain,
    w_query,
    w_key,
    w_value,
    w_score,
):
    n_corpus = lax.axis_size("corpus")
    n_rerank = lax.axis_size("rerank")
    corpus_index = lax.axis_index("corpus")
    member = lax.axis_index("rerank")
    pair_total = cand_block.shape[0]
    pair_group = pair_total // n_corpus
    pair_dev = pair_group // n_rerank
    own_blocks = store_rows.shape[0]
    owners = cand_owner[:, 0]
    pair_order = jnp.arange(pair_total, dtype=jnp.int32)
    group_of = pair_order // pair_group
    earlier = (
        (owners[:, None] == owners[None, :])
        & (group_of[:, None] == group_of[None, :])
        & (pair_order[None, :] < pair_order[:, None])
    )
    owner_rank = jnp.sum(earlier.astype(jnp.int32), axis=1)
    slot_ids = jnp.arange(n_corpus * CAP, dtype=jnp.int32)
    slot_group = slot_ids // CAP
    slot_rank = slot_ids % CAP
    wanted = (
        (group_of[None, :] == slot_group[:, None])
        & (owners[None, :] == corpus_index)
        & (owner_rank[None, :] == slot_rank[:, None])
    )
    outgoing = pick_rows(store_rows, wanted, cand_block)
    arrived = lax.all_to_all(outgoing, "corpus", split_axis=0, concat_axis=0, tiled=True)
    local_pairs = corpus_index * pair_group + jnp.arange(pair_group, dtype=jnp.int32)
    local_owner = jnp.take(owners, local_pairs)
    local_rank = jnp.take(owner_rank, local_pairs)
    passages = jnp.take(arrived, local_owner * CAP + local_rank, axis=0)
    query_rows = jnp.take(queries, jnp.take(cand_query, local_pairs), axis=0)
    passage_rows, question_rows = (
        lax.all_to_all(passages, "rerank", split_axis=0, concat_axis=1, tiled=True),
        lax.all_to_all(query_rows, "rerank", split_axis=0, concat_axis=1, tiled=True),
    )
    joined = jnp.concatenate([passage_rows, question_rows], axis=1)
    device_pairs = (
        corpus_index * pair_group + member * pair_dev + jnp.arange(pair_dev, dtype=jnp.int32)
    )
    lengths = jnp.take(
        block_lengths,
        jnp.take(owners, device_pairs) * own_blocks + jnp.take(cand_block, device_pairs),
    )
    seq_len = joined.shape[1]
    width = joined.shape[2]
    row_count = pair_dev * seq_len
    widened = joined.astype(jnp.float32)
    inverse_rms = lax.rsqrt(jnp.mean(widened * widened, axis=-1, keepdims=True) + EPSILON)
    normed = (
        (widened * inverse_rms * norm_gain.astype(jnp.float32))
        .astype(jnp.bfloat16)
        .reshape(row_count, width)
    )
    query_raw, key_raw, value_raw = add_products(
        (
            lax.all_gather(w_query, "rerank", axis=0, tiled=True),
            lax.all_gather(w_key, "rerank", axis=0, tiled=True),
            lax.all_gather(w_value, "rerank", axis=0, tiled=True),
        ),
        normed,
    )
    token_ids = jnp.arange(seq_len, dtype=jnp.int32)
    positions = jnp.where(
        token_ids[None, :] < BLK, token_ids[None, :], lengths[:, None] + token_ids[None, :] - BLK
    )
    query_rot = rotate(query_raw.reshape(pair_dev, seq_len, QHEADS, HDIM), positions).astype(
        jnp.bfloat16
    )
    key_rot = rotate(key_raw.reshape(pair_dev, seq_len, KVHEADS, HDIM), positions).astype(
        jnp.bfloat16
    )
    values = value_raw.reshape(pair_dev, seq_len, KVHEADS, HDIM).astype(jnp.bfloat16)
    context = lax.map(attend_one, (query_rot, key_rot, values, lengths))
    pair_scores = jnp.dot(context[:, seq_len - 1, :], w_score, preferred_element_type=jnp.float32)
    keep = token_ids[None, :BLK] < lengths[:, None]
    passage_context = jnp.where(keep[:, :, None], context[:, :BLK], jnp.zeros((), jnp.bfloat16))
    returned = lax.all_to_all(passage_context, "rerank", split_axis=1, concat_axis=0, tiled=True)
    home_want = (local_owner[None, :] == slot_group[:, None]) & (
        local_rank[None, :] == slot_rank[:, None]
    )
    homebound = pick_rows(returned, home_want, jnp.arange(pair_group, dtype=jnp.int32))
    landed = lax.all_to_all(homebound, "corpus", split_axis=0, concat_axis=0, tiled=True)
    return (landed, pair_scores)


def solution(mesh):
    placed = (
        P("corpus", "rerank", None),
        P(),
        P(None, "rerank", None),
        P(),
        P(),
        P(),
        P(),
        P("rerank", None),
        P("rerank", None),
        P("rerank", None),
        P(),
    )
    return jax.shard_map(
        on_device,
        mesh=mesh,
        in_specs=placed,
        out_specs=(P("corpus", "rerank", None), P(("corpus", "rerank"))),
        check_vma=False,
    )
```

profile of v0, /device:TPU:2, one launch (start us, length us, event | category | flops | bytes accessed | tf_op | source)
XLA Modules:
  0.0 673.4 jit_solution(5403517321702879606)
XLA Ops:
  9.4 0.9 convert_reduce_fusion
  10.3 0.8 select_reduce_fusion
  11.4 11.1 %gather_fusion.1 = bf16[20,64,3584]{2,1,0:T(8,128)(2,1)} fusion(bf16[32,64,3584]{2,1,0:T(8,128)(2,1)} %param.17, s32[1024]{0:T(1024)S(1)} %pad_clamp_fusion.3), kind=kCustom, calls=%fused_computation.6 | custom fusion | bytes 18350160 | tf_op jit(solution)/shard_map/jit(_take)/gather | solution.py:32
  22.5 8.2 %select_select_fusion = bf16[20,64,3584]{2,1,0:T(8,128)(2,1)} fusion(bf16[20,64,3584]{2,1,0:T(8,128)(2,1)} %gather_fusion.1, pred[20]{0:T(512)(128)(4,1)S(1)} %compare_and_fusion.5, pred[20]{0:T(512)(128)(4,1)S(1)} %fusion.35), kind=kLoop, calls=%fused_computation.45 | loop fusion | flops 9175040 | bytes 18350120 | tf_op jit(solution)/shard_map/jit(_where)/select_n | solution.py:33
  30.7 5.9 all-to-all-start
  40.6 1.1 broadcast_select_fusion.2
  41.7 195.2 %all-to-all-done = bf16[20,64,3584]{2,1,0:T(8,128)(2,1)} async-done(((bf16[20,64,3584]{2,1,0:T(8,128)(2,1)}), bf16[20,64,3584]{2,1,0:T(8,128)(2,1)}, u32[]{:S(2)}, u32[]{:S(2)}) %all-to-all-start) | async-done | bytes 9175072 | tf_op jit(solution)/shard_map/all_to_all | solution.py:101
  236.8 4.2 all-to-all-start.2
  241.1 7.6 %gather_fusion.2 = bf16[16,64,3584]{2,1,0:T(8,128)(2,1)} fusion(bf16[20,64,3584]{2,1,0:T(8,128)(2,1)} %all-to-all-done, s32[1024]{0:T(1024)S(1)} %pad_clamp_fusion.2), kind=kCustom, calls=%fused_computation.7 | custom fusion | bytes 14680128 | tf_op jit(solution)/shard_map/jit(_take)/gather | solution.py:105
  248.7 6.9 %broadcast_select_fusion = bf16[16,64,3584]{2,1,0:T(8,128)(2,1)} fusion(bf16[16,64,3584]{2,1,0:T(8,128)(2,1)} %gather_fusion.2, pred[16]{0:T(512)(128)(4,1)S(1)} %get-tuple-element.63), kind=kLoop, calls=%fused_computation.50 | loop fusion | flops 3670016 | bytes 14680080 | tf_op jit(solution)/shard_map/jit(_take)/select_n | solution.py:105
  255.6 5.2 all-to-all-start.1
  263.7 2.1 multiply_cosine_fusion
  265.8 1.0 copy.62
  266.8 3.8 copy.49
  270.6 3.8 copy.48
  274.4 67.8 %all-to-all-done.1 = bf16[16,64,3584]{2,1,0:T(8,128)(2,1)} async-done(((bf16[16,64,3584]{2,1,0:T(8,128)(2,1)}), bf16[16,64,3584]{2,1,0:T(8,128)(2,1)}, u32[]{:S(2)}, u32[]{:S(2)}) %all-to-all-start.1) | async-done | bytes 7340064 | tf_op jit(solution)/shard_map/all_to_all | solution.py:108
  342.2 3.8 copy.46
  346.0 2.0 fusion.30
  348.9 2.4 fusion.41
  352.1 3.4 convolution_convert_fusion
  355.5 18.0 %copy.50 = bf16[1792,3584]{1,0:T(8,128)(2,1)} copy(bf16[1792,3584]{0,1:T(8,128)(2,1)} %bitcast.115) | data formatting | bytes 25690112 | tf_op jit(solution)/shard_map/dot_general | solution.py:38
  373.5 23.9 %fusion.39 = f32[2,576,14,128]{3,1,2,0:T(8,128)} fusion(bf16[14,128,3584,1]{2,1,0,3:T(8,128)(2,1)} %bitcast.116, f32[3584]{0:T(1024)S(1)} %convert_element_type.66, f32[2,576]{1,0:T(2,128)S(1)} %add_rsqrt_fusion, bf16[2,64,3584]{2,1,0:T(8,128)(2,1)S(1)} %bitcast.121, bf16[2,512,3584]{2,1,0:T(8,128)(2,1)} %bitcast.112), kind=kOutput, calls=%fused_computation.117 | convolution fusion | flops 14826405888 | bytes 29379072 | tf_op jit(solution)/shard_map/dot_general | solution.py:38
  397.4 8.6 %subtract_convert_fusion = (bf16[2,576,14,64]{3,1,2,0:T(8,128)(2,1)S(1)}, bf16[2,576,14,64]{3,1,2,0:T(8,128)(2,1)S(1)}) fusion(f32[2,576,14,128]{3,1,2,0:T(8,128)} %fusion.39, f32[2,576,64]{2,1,0:T(8,128)S(1)} %get-tuple-element.62, f32[2,576,64]{2,1,0:T(8,128)S(1)} %get-tuple-element.61), kind=kLoop, calls=%fused_computation.49 | loop fusion | flops 8257536 | bytes 12976128 | tf_op jit(solution)/shard_map/convert.2
  405.9 4.3 pad_maximum_fusion.1
  410.2 69.3 %while.10 = (s32[]{:T(128)}, bf16[2,576,1792]{2,1,0:T(8,128)(2,1)}, bf16[2,576,2,128]{3,1,2,0:T(8,128)(2,1)}, s32[2]{0:T(128)S(1)}, bf16[2,576,2,128]{3,1,2,0:T(...) while((s32[]{:T(128)}, bf16[2,576,1792]{2,1,0:T(8,128)(2,1)}, ...), condition=%wide.region_9.12_spmd, body=%wide.region_6.11_spmd.sunk | while | flops 2412382464 | bytes 61592804 | solution.py:148
  410.4 1.7 constant_dynamic-slice_fusion.2
  413.5 12.5 %fusion.66 = (f32[2,7,576]{2,1,0:T(8,128)S(1)}, f32[2,7,576,576]{2,3,1,0:T(8,128)}) fusion(pred[576,576]{0,1:T(8,128)(4,1)S(1)} %fusion.65, bf16[576,2,7,128]{3,0,2,1:T(8,128)(2,1)S(1)} %bitcast.108, bf16[2,576,2,128]{3,1,2,0:T(8,128)(2,1)S(1)} %get-tuple-element.128, s32[]{:T(128)} %get-tuple-element.117), kind=kOutput, calls=%fused_computation.119.clone.1 | convolution fusion | flops 1212310016 | bytes 21708292 | tf_op jit(solution)/shard_map/while/body/eval_jaxpr/sub | solution.py:56
  426.0 11.1 %convert_bitcast_fusion.2 = bf16[576,2,7,128]{3,0,2,1:T(8,128)(2,1)S(1)} fusion(f32[2,7,576,576]{2,3,1,0:T(8,128)} %get-tuple-element.108, f32[2,7,576]{2,1,0:T(8,128)S(1)} %get-tuple-element.109, bf16[2,576,2,128]{3,1,2,0:T(8,128)(2,1)} %get-tuple-element.126, s32[]{:T(128)} %get-tuple-element.117), kind=kOutput, calls=%fused_computation.19.clone.1 | convolution fusion | flops 1199407104 | bytes 23035904 | tf_op jit(solution)/shard_map/while/body/eval_jaxpr/kgst,tkd->skgd/dot_general | solution.py:58
  437.1 1.4 copy.64
  438.5 3.3 convert_element_type.102
  441.8 3.0 constant_dynamic-update-slice_fusion.2
  444.8 1.7 constant_dynamic-slice_fusion.2
  448.0 12.5 %fusion.66 = (f32[2,7,576]{2,1,0:T(8,128)S(1)}, f32[2,7,576,576]{2,3,1,0:T(8,128)}) fusion(pred[576,576]{0,1:T(8,128)(4,1)S(1)} %fusion.65, bf16[576,2,7,128]{3,0,2,1:T(8,128)(2,1)S(1)} %bitcast.108, bf16[2,576,2,128]{3,1,2,0:T(8,128)(2,1)S(1)} %get-tuple-element.128, s32[]{:T(128)} %get-tuple-element.117), kind=kOutput, calls=%fused_computation.119.clone.1 | convolution fusion | flops 1212310016 | bytes 21708292 | tf_op jit(solution)/shard_map/while/body/eval_jaxpr/sub | solution.py:56
  460.5 11.1 %convert_bitcast_fusion.2 = bf16[576,2,7,128]{3,0,2,1:T(8,128)(2,1)S(1)} fusion(f32[2,7,576,576]{2,3,1,0:T(8,128)} %get-tuple-element.108, f32[2,7,576]{2,1,0:T(8,128)S(1)} %get-tuple-element.109, bf16[2,576,2,128]{3,1,2,0:T(8,128)(2,1)} %get-tuple-element.126, s32[]{:T(128)} %get-tuple-element.117), kind=kOutput, calls=%fused_computation.19.clone.1 | convolution fusion | flops 1199407104 | bytes 23035904 | tf_op jit(solution)/shard_map/while/body/eval_jaxpr/kgst,tkd->skgd/dot_general | solution.py:58
  471.6 1.4 copy.64
  473.0 3.3 convert_element_type.102
  476.3 3.0 constant_dynamic-update-slice_fusion.2
  479.5 6.4 copy.51
  486.0 5.7 broadcast_select_fusion.1
  491.7 5.9 all-to-all-start.3
  497.8 41.8 %all-to-all-done.3 = bf16[2,512,1792]{2,0,1:T(2,128)(2,1)} async-done(((bf16[2,512,1792]{2,0,1:T(2,128)(2,1)}), bf16[2,512,1792]{2,0,1:T(2,128)(2,1)}, u32[]{:S(2)}, u32[]{:S(2)}) %all-to-all-start.3) | async-done | bytes 3670048 | tf_op jit(solution)/shard_map/all_to_all | solution.py:152
  539.7 2.5 copy.52
  542.2 2.1 copy.53
  544.3 5.3 gather_fusion.4
  549.5 5.1 select_select_fusion.1
  554.7 4.9 all-to-all-start.4
  561.1 100.6 %all-to-all-done.4 = bf16[20,64,1792]{2,1,0:T(8,128)(2,1)} async-done(((bf16[20,64,1792]{2,1,0:T(8,128)(2,1)}), bf16[20,64,1792]{2,1,0:T(8,128)(2,1)}, u32[]{:S(2)}, u32[]{:S(2)}) %all-to-all-start.4) | async-done | bytes 4587552 | tf_op jit(solution)/shard_map/all_to_all | solution.py:157
  661.8 4.9 copy.75
  (97 shorter events, 15.3 us)
Async XLA Ops:
  7.2 32.8 %copy-start = (bf16[32,8,3584]{2,1,0:T(8,128)(2,1)S(1)}, bf16[32,8,3584]{2,1,0:T(8,128)(2,1)}, u32[]{:S(2)}) copy-start(bf16[32,8,3584]{2,1,0:T(8,128)(2,1)} %param.19) | copy-start | bytes 5505028
  7.2 259.6 %all-gather.6.cloned.1.call-start = ((), (), s32[]{:S(2)}) async-start(), calls=%async_computation.6 | async-start | bytes 2064384 | tf_op jit(solution)/shard_map/all_gather | solution.py:132
  7.9 262.7 %all-gather.4.cloned.1.call-start = ((), (), s32[]{:S(2)}) async-start(), calls=%async_computation.5 | async-start | bytes 2064384 | tf_op jit(solution)/shard_map/all_gather | solution.py:133
  8.7 13.8 %copy-start.12 = (s32[20]{0:T(128)}, s32[20]{0:T(128)S(1)}, u32[]{:S(2)}) copy-start(s32[20]{0:T(128)S(1)} %get-tuple-element.67) | copy-start | bytes 244
  8.7 13.8 %copy-start.14 = (s32[20]{0:T(128)}, s32[20]{0:T(128)S(1)}, u32[]{:S(2)}) copy-start(s32[20]{0:T(128)S(1)} %get-tuple-element.68) | copy-start | bytes 244
  30.7 7.3 %copy-start.2 = (s32[64,1]{0,1:T(1,128)S(1)}, s32[64,1]{0,1:T(1,128)}, u32[]{:S(2)}) copy-start(s32[64,1]{0,1:T(1,128)} %param.20) | copy-start | bytes 772
  30.7 8.0 %copy-start.4 = (s32[64]{0:T(128)S(1)}, s32[64]{0:T(128)}, u32[]{:S(2)}) copy-start(s32[64]{0:T(128)} %param.22) | copy-start | bytes 772
  30.7 206.1 %all-to-all-start = ((bf16[20,64,3584]{2,1,0:T(8,128)(2,1)}), bf16[20,64,3584]{2,1,0:T(8,128)(2,1)}, u32[]{:S(2)}, u32[]{:S(2)}) async-start(bf16[20,64,3584]{2,1,0:T(8,128)(2,1)} %select_select_fusion), calls=%async_computation | async-start | bytes 18350080 | tf_op jit(solution)/shard_map/all_to_all | solution.py:101
  36.6 318.9 %all-gather.8.cloned.1.call-start = ((), (), s32[]{:S(2)}) async-start(), calls=%async_computation.7 | async-start | bytes 14450688 | tf_op jit(solution)/shard_map/all_gather | solution.py:131
  236.8 18.7 %all-to-all-start.2 = ((bf16[16,8,3584]{2,1,0:T(8,128)(2,1)}), bf16[16,8,3584]{2,1,0:T(8,128)(2,1)S(1)}, u32[]{:S(2)}, u32[]{:S(2)}) async-start(bf16[16,8,3584]{2,1,0:T(8,128)(2,1)} %broadcast_select_fusion.2), calls=%async_computation.2 | async-start | bytes 1835008 | tf_op jit(solution)/shard_map/all_to_all | solution.py:109
  255.6 5.9 copy-start.3
  255.6 6.6 copy-start.11
  255.6 6.6 copy-start.5
  255.6 86.6 %all-to-all-start.1 = ((bf16[16,64,3584]{2,1,0:T(8,128)(2,1)}), bf16[16,64,3584]{2,1,0:T(8,128)(2,1)}, u32[]{:S(2)}, u32[]{:S(2)}) async-start(bf16[16,64,3584]{2,1,0:T(8,128)(2,1)} %broadcast_select_fusion), calls=%async_computation.1 | async-start | bytes 14680064 | tf_op jit(solution)/shard_map/all_to_all | solution.py:108
  342.2 3.8 copy-start.7
  346.0 6.1 copy-start.6
  346.0 2.9 copy-start.9
  348.9 3.2 copy-start.8
  479.5 6.5 copy-start.10
  486.0 11.6 %copy-start.13 = (s32[20]{0:T(128)S(1)}, s32[20]{0:T(128)}, u32[]{:S(2)}) copy-start(s32[20]{0:T(128)} %copy-done.12) | copy-start | bytes 244
  486.0 11.6 %copy-start.15 = (s32[20]{0:T(128)S(1)}, s32[20]{0:T(128)}, u32[]{:S(2)}) copy-start(s32[20]{0:T(128)} %copy-done.14) | copy-start | bytes 244
  486.0 11.6 %copy-start.16 = (s32[16]{0:T(128)S(1)}, s32[16]{0:T(128)}, u32[]{:S(2)}) copy-start(s32[16]{0:T(128)} %get-tuple-element.65) | copy-start | bytes 196
  486.0 11.6 %copy-start.17 = (s32[16]{0:T(128)S(1)}, s32[16]{0:T(128)}, u32[]{:S(2)}) copy-start(s32[16]{0:T(128)} %get-tuple-element.66) | copy-start | bytes 196
  491.7 48.0 %all-to-all-start.3 = ((bf16[2,512,1792]{2,0,1:T(2,128)(2,1)}), bf16[2,512,1792]{2,0,1:T(2,128)(2,1)}, u32[]{:S(2)}, u32[]{:S(2)}) async-start(bf16[2,512,1792]{2,0,1:T(2,128)(2,1)} %broadcast_select_fusion.1), calls=%async_computation.3 | async-start | bytes 7340032 | tf_op jit(solution)/shard_map/all_to_all | solution.py:152
  549.5 10.1 %copy-start.18 = (bf16[1792]{0:T(1024)(128)(2,1)S(1)}, bf16[1792]{0:T(1024)(128)(2,1)}, u32[]{:S(2)}) copy-start(bf16[1792]{0:T(1024)(128)(2,1)} %param.27) | copy-start | bytes 10756
  549.5 117.1 %copy-start.1 = (bf16[32,8,3584]{2,1,0:T(8,128)(2,1)S(1)}, bf16[32,8,3584]{2,1,0:T(8,128)(2,1)}, u32[]{:S(2)}) copy-start(bf16[32,8,3584]{2,1,0:T(8,128)(2,1)} %param.19) | copy-start | bytes 5505028
  554.7 107.1 %all-to-all-start.4 = ((bf16[20,64,1792]{2,1,0:T(8,128)(2,1)}), bf16[20,64,1792]{2,1,0:T(8,128)(2,1)}, u32[]{:S(2)}, u32[]{:S(2)}) async-start(bf16[20,64,1792]{2,1,0:T(8,128)(2,1)} %select_select_fusion.1), calls=%async_computation.4 | async-start | bytes 9175040 | tf_op jit(solution)/shard_map/all_to_all | solution.py:157
Sparse Core Ops, SparseCore 0:
  9.9 27.8 all-gather.5
  39.7 26.6 all-gather.3
  68.3 73.0 all-gather.7
where the time goes:
time: 679 us; the launch traced here: 673 us
  waiting for transfers between devices  407 us (60%)
  local copies, waits for them, and re-layouts  96.6 us (14%)
  matrix products  77.5 us (11%)
  other arithmetic  50.7 us (7%)
  starting transfers between devices  26.3 us (4%)
  between operations  14.4 us (2%)
    all_to_all x1, waiting for transfers between devices, on_device(): lax.all_to_all(outgoing, 'corpus', split_axis=0, concat_axis=0, tiled=True)  195 us
    all_to_all x1, waiting for transfers between devices, on_device(): lax.all_to_all(homebound, 'corpus', split_axis=0, concat_axis=0, tiled=True)  101 us
    all_to_all x1, waiting for transfers between devices, on_device(): lax.all_to_all(passages, 'rerank', split_axis=0, concat_axis=1, tiled=True)  67.8 us
    all_to_all x1, waiting for transfers between devices, on_device(): lax.all_to_all(passage_context, 'rerank', split_axis=1, concat_axis=0, ti...  41.8 us
    sub x2, matrix products, attend_one(): weights = jnp.where(allowed, jnp.exp(masked - peak), 0.0)  25 us
    dot_general x1, matrix products, add_products(): jnp.dot(columns, pieces[0], preferred_element_type=jnp.float32)  23.9 us
    dot_general x2, matrix products, attend_one(): jnp.einsum('kgst,tkd->skgd', probs, values, preferred_element_type=jnp.fl...  22.2 us
    dot_general x1, local copies, waits for them, and re-layouts, add_products(): jnp.dot(columns, pieces[0], preferred_element_type=jnp.float32)  18 us
  transfers between devices with their start and end apart: 8, of which 4 were waited for; matrix products, arithmetic and copies ran while one was open for 10% of the time, Pallas kernels for 0%

commit v1 on v0

--- a/solution.py
+++ b/solution.py
@@ -10,6 +10,22 @@
 CAP = 5
 ROPE_BASE = 1000000.0
 EPSILON = 1e-06
+
+
+def exchange_in_pairs(value, axis, split, join):
+    ways, here = (lax.axis_size(axis), lax.axis_index(axis))
+    width = value.shape[split] // ways
+    dims = list(value.shape)
+    dims[split] = width
+    height = dims[join]
+    dims[join] = height * ways
+    full = jnp.zeros(dims, value.dtype)
+    for mask in range(ways):
+        part = lax.dynamic_slice_in_dim(value, (here ^ mask) * width, width, axis=split)
+        if mask:
+            part = lax.ppermute(part, axis, [(d, d ^ mask) for d in range(ways)])
+        full = lax.dynamic_update_slice_in_dim(full, part, (here ^ mask) * height, axis=join)
+    return full
 
 
 def rotate(values, positions):
@@ -154,7 +170,7 @@
         local_rank[None, :] == slot_rank[:, None]
     )
     homebound = pick_rows(returned, home_want, jnp.arange(pair_group, dtype=jnp.int32))
-    landed = lax.all_to_all(homebound, "corpus", split_axis=0, concat_axis=0, tiled=True)
+    landed = exchange_in_pairs(homebound, "corpus", 0, 0)
     return (landed, pair_scores)
 
 

time: 679 us -> 670 us (0.987)
  the two profiles are of different devices: /device:TPU:2 before, /device:TPU:10 now
where the time goes in v1:
time: 670 us; the launch traced here: 664 us
  waiting for transfers between devices  401 us (60%)
  local copies, waits for them, and re-layouts  95.8 us (14%)
  matrix products  77.5 us (12%)
  other arithmetic  48.4 us (7%)
  starting transfers between devices  26.7 us (4%)
  between operations  14.4 us (2%)
    all_to_all x1, waiting for transfers between devices, on_device(): lax.all_to_all(outgoing, 'corpus', split_axis=0, concat_axis=0, tiled=True)  192 us
    ppermute x3, waiting for transfers between devices, exchange_in_pairs(): part = lax.ppermute(part, axis, [(d, d ^ mask) for d in range(ways)])  97.3 us
    all_to_all x1, waiting for transfers between devices, on_device(): lax.all_to_all(passages, 'rerank', split_axis=0, concat_axis=1, tiled=True)  67.7 us
    all_to_all x1, waiting for transfers between devices, on_device(): lax.all_to_all(passage_context, 'rerank', split_axis=1, concat_axis=0, ti...  41.8 us
    sub x2, matrix products, attend_one(): weights = jnp.where(allowed, jnp.exp(masked - peak), 0.0)  25 us
    dot_general x1, matrix products, add_products(): jnp.dot(columns, pieces[0], preferred_element_type=jnp.float32)  23.9 us
    dot_general x2, matrix products, attend_one(): jnp.einsum('kgst,tkd->skgd', probs, values, preferred_element_type=jnp.fl...  22.2 us
    dot_general x1, local copies, waits for them, and re-layouts, add_products(): jnp.dot(columns, pieces[0], preferred_element_type=jnp.float32)  18 us
  transfers between devices with their start and end apart: 10, of which 6 were waited for; matrix products, arithmetic and copies ran while one was open for 10% of the time, Pallas kernels for 0%

profile of v1, /device:TPU:10, one launch (start us, length us, event | category | flops | bytes accessed | tf_op | source)
XLA Modules:
  0.0 664.0 jit_solution(15614570440842747529)
XLA Ops:
  11.4 11.1 %gather_fusion.1 = bf16[20,64,3584]{2,1,0:T(8,128)(2,1)} fusion(bf16[32,64,3584]{2,1,0:T(8,128)(2,1)} %param.17, s32[1024]{0:T(1024)S(1)} %pad_clamp_fusion.3), kind=kCustom, calls=%fused_computation.6 | custom fusion | bytes 18350160 | tf_op jit(solution)/shard_map/jit(_take)/gather | solution.py:48
  22.5 8.2 %select_select_fusion = bf16[20,64,3584]{2,1,0:T(8,128)(2,1)} fusion(bf16[20,64,3584]{2,1,0:T(8,128)(2,1)} %gather_fusion.1, pred[20]{0:T(512)(128)(4,1)S(1)} %compare_and_fusion.5, pred[20]{0:T(512)(128)(4,1)S(1)} %fusion.35), kind=kLoop, calls=%fused_computation.45 | loop fusion | flops 9175040 | bytes 18350120 | tf_op jit(solution)/shard_map/jit(_where)/select_n | solution.py:49
  30.7 6.3 all-to-all-start
  41.0 1.1 broadcast_select_fusion.2
  42.0 191.8 %all-to-all-done = bf16[20,64,3584]{2,1,0:T(8,128)(2,1)} async-done(((bf16[20,64,3584]{2,1,0:T(8,128)(2,1)}), bf16[20,64,3584]{2,1,0:T(8,128)(2,1)}, u32[]{:S(2)}, u32[]{:S(2)}) %all-to-all-start) | async-done | bytes 9175072 | tf_op jit(solution)/shard_map/all_to_all | solution.py:117
  233.9 4.2 all-to-all-start.2
  238.1 7.6 %gather_fusion.2 = bf16[16,64,3584]{2,1,0:T(8,128)(2,1)} fusion(bf16[20,64,3584]{2,1,0:T(8,128)(2,1)} %all-to-all-done, s32[1024]{0:T(1024)S(1)} %pad_clamp_fusion.2), kind=kCustom, calls=%fused_computation.7 | custom fusion | bytes 14680128 | tf_op jit(solution)/shard_map/jit(_take)/gather | solution.py:121
  245.7 6.8 %broadcast_select_fusion = bf16[16,64,3584]{2,1,0:T(8,128)(2,1)} fusion(bf16[16,64,3584]{2,1,0:T(8,128)(2,1)} %gather_fusion.2, pred[16]{0:T(512)(128)(4,1)S(1)} %get-tuple-element.67), kind=kLoop, calls=%fused_computation.50 | loop fusion | flops 3670016 | bytes 14680080 | tf_op jit(solution)/shard_map/jit(_take)/select_n | solution.py:121
  252.6 5.2 all-to-all-start.1
  260.7 2.1 multiply_cosine_fusion
  263.8 3.8 copy.49
  267.7 3.8 copy.48
  271.5 67.7 %all-to-all-done.1 = bf16[16,64,3584]{2,1,0:T(8,128)(2,1)} async-done(((bf16[16,64,3584]{2,1,0:T(8,128)(2,1)}), bf16[16,64,3584]{2,1,0:T(8,128)(2,1)}, u32[]{:S(2)}, u32[]{:S(2)}) %all-to-all-start.1) | async-done | bytes 7340064 | tf_op jit(solution)/shard_map/all_to_all | solution.py:124
  339.2 3.8 copy.46
  343.0 2.0 fusion.30
  345.9 2.4 fusion.41
  349.8 3.4 convolution_convert_fusion
  353.2 18.0 %copy.50 = bf16[1792,3584]{1,0:T(8,128)(2,1)} copy(bf16[1792,3584]{0,1:T(8,128)(2,1)} %bitcast.115) | data formatting | bytes 25690112 | tf_op jit(solution)/shard_map/dot_general | solution.py:54
  371.1 23.9 %fusion.39 = f32[2,576,14,128]{3,1,2,0:T(8,128)} fusion(bf16[14,128,3584,1]{2,1,0,3:T(8,128)(2,1)} %bitcast.116, f32[3584]{0:T(1024)S(1)} %convert_element_type.66, f32[2,576]{1,0:T(2,128)S(1)} %add_rsqrt_fusion, bf16[2,64,3584]{2,1,0:T(8,128)(2,1)S(1)} %bitcast.121, bf16[2,512,3584]{2,1,0:T(8,128)(2,1)} %bitcast.112), kind=kOutput, calls=%fused_computation.124 | convolution fusion | flops 14826405888 | bytes 29379072 | tf_op jit(solution)/shard_map/dot_general | solution.py:54
  395.0 8.6 %subtract_convert_fusion = (bf16[2,576,14,64]{3,1,2,0:T(8,128)(2,1)S(1)}, bf16[2,576,14,64]{3,1,2,0:T(8,128)(2,1)S(1)}) fusion(f32[2,576,14,128]{3,1,2,0:T(8,128)} %fusion.39, f32[2,576,64]{2,1,0:T(8,128)S(1)} %get-tuple-element.66, f32[2,576,64]{2,1,0:T(8,128)S(1)} %get-tuple-element.65), kind=kLoop, calls=%fused_computation.49 | loop fusion | flops 8257536 | bytes 12976128 | tf_op jit(solution)/shard_map/convert.2
  403.6 4.3 pad_maximum_fusion.1
  407.9 69.3 %while.10 = (s32[]{:T(128)}, bf16[2,576,1792]{2,1,0:T(8,128)(2,1)}, bf16[2,576,2,128]{3,1,2,0:T(8,128)(2,1)}, s32[2]{0:T(128)S(1)}, bf16[2,576,2,128]{3,1,2,0:T(...) while((s32[]{:T(128)}, bf16[2,576,1792]{2,1,0:T(8,128)(2,1)}, ...), condition=%wide.region_9.12_spmd, body=%wide.region_6.11_spmd.sunk | while | flops 2412382464 | bytes 61592804 | solution.py:164
  408.0 1.7 constant_dynamic-slice_fusion.5
  411.2 12.5 %fusion.66 = (f32[2,7,576]{2,1,0:T(8,128)S(1)}, f32[2,7,576,576]{2,3,1,0:T(8,128)}) fusion(pred[576,576]{0,1:T(8,128)(4,1)S(1)} %fusion.65, bf16[576,2,7,128]{3,0,2,1:T(8,128)(2,1)S(1)} %bitcast.108, bf16[2,576,2,128]{3,1,2,0:T(8,128)(2,1)S(1)} %get-tuple-element.132, s32[]{:T(128)} %get-tuple-element.121), kind=kOutput, calls=%fused_computation.126.clone.1 | convolution fusion | flops 1212310016 | bytes 21708292 | tf_op jit(solution)/shard_map/while/body/eval_jaxpr/sub | solution.py:72
  423.7 11.1 %convert_bitcast_fusion.2 = bf16[576,2,7,128]{3,0,2,1:T(8,128)(2,1)S(1)} fusion(f32[2,7,576,576]{2,3,1,0:T(8,128)} %get-tuple-element.112, f32[2,7,576]{2,1,0:T(8,128)S(1)} %get-tuple-element.113, bf16[2,576,2,128]{3,1,2,0:T(8,128)(2,1)} %get-tuple-element.130, s32[]{:T(128)} %get-tuple-element.121), kind=kOutput, calls=%fused_computation.19.clone.1 | convolution fusion | flops 1199407104 | bytes 23035904 | tf_op jit(solution)/shard_map/while/body/eval_jaxpr/kgst,tkd->skgd/dot_general | solution.py:74
  434.8 1.4 copy.64
  436.2 3.3 convert_element_type.102
  439.5 3.0 constant_dynamic-update-slice_fusion.5
  442.5 1.7 constant_dynamic-slice_fusion.5
  445.7 12.5 %fusion.66 = (f32[2,7,576]{2,1,0:T(8,128)S(1)}, f32[2,7,576,576]{2,3,1,0:T(8,128)}) fusion(pred[576,576]{0,1:T(8,128)(4,1)S(1)} %fusion.65, bf16[576,2,7,128]{3,0,2,1:T(8,128)(2,1)S(1)} %bitcast.108, bf16[2,576,2,128]{3,1,2,0:T(8,128)(2,1)S(1)} %get-tuple-element.132, s32[]{:T(128)} %get-tuple-element.121), kind=kOutput, calls=%fused_computation.126.clone.1 | convolution fusion | flops 1212310016 | bytes 21708292 | tf_op jit(solution)/shard_map/while/body/eval_jaxpr/sub | solution.py:72
  458.2 11.1 %convert_bitcast_fusion.2 = bf16[576,2,7,128]{3,0,2,1:T(8,128)(2,1)S(1)} fusion(f32[2,7,576,576]{2,3,1,0:T(8,128)} %get-tuple-element.112, f32[2,7,576]{2,1,0:T(8,128)S(1)} %get-tuple-element.113, bf16[2,576,2,128]{3,1,2,0:T(8,128)(2,1)} %get-tuple-element.130, s32[]{:T(128)} %get-tuple-element.121), kind=kOutput, calls=%fused_computation.19.clone.1 | convolution fusion | flops 1199407104 | bytes 23035904 | tf_op jit(solution)/shard_map/while/body/eval_jaxpr/kgst,tkd->skgd/dot_general | solution.py:74
  469.3 1.4 copy.64
  470.6 3.3 convert_element_type.102
  474.0 3.0 constant_dynamic-update-slice_fusion.5
  477.2 6.4 copy.51
  483.6 5.7 broadcast_select_fusion.1
  489.3 5.9 all-to-all-start.3
  495.5 41.8 %all-to-all-done.3 = bf16[2,512,1792]{2,0,1:T(2,128)(2,1)} async-done(((bf16[2,512,1792]{2,0,1:T(2,128)(2,1)}), bf16[2,512,1792]{2,0,1:T(2,128)(2,1)}, u32[]{:S(2)}, u32[]{:S(2)}) %all-to-all-start.3) | async-done | bytes 3670048 | tf_op jit(solution)/shard_map/all_to_all | solution.py:168
  537.3 2.5 copy.52
  539.8 2.1 copy.53
  541.9 5.3 gather_fusion.4
  547.2 2.9 select_select_fusion.1
  551.0 3.5 collective-permute-start
  554.5 1.5 collective-permute-start.2
  557.5 45.1 %collective-permute-done = bf16[5,64,1792]{2,1,0:T(8,128)(2,1)S(1)} collective-permute-done((bf16[5,64,1792]{2,1,0:T(8,128)(2,1)S(1)}, bf16[5,64,1792]{2,1,0:T(8,128)(2,1)S(1)}, u32[]{:S(2)}, u32[]{:S(2)}) %collective-permute-start) | collective-permute-done | bytes 1146912 | tf_op jit(solution)/shard_map/ppermute | solution.py:26
  602.7 26.7 %collective-permute-done.1 = bf16[5,64,1792]{2,1,0:T(8,128)(2,1)S(1)} collective-permute-done((bf16[5,64,1792]{2,1,0:T(8,128)(2,1)S(1)}, bf16[5,64,1792]{2,1,0:T(8,128)(2,1)S(1)}, u32[]{:S(2)}, u32[]{:S(2)}) %collective-permute-start.1) | collective-permute-done | bytes 1146912 | tf_op jit(solution)/shard_map/ppermute | solution.py:26
  629.5 25.5 %collective-permute-done.2 = bf16[5,64,1792]{2,1,0:T(8,128)(2,1)S(1)} collective-permute-done((bf16[5,64,1792]{2,1,0:T(8,128)(2,1)S(1)}, bf16[5,64,1792]{2,1,0:T(8,128)(2,1)S(1)}, u32[]{:S(2)}, u32[]{:S(2)}) %collective-permute-start.2) | collective-permute-done | bytes 1146912 | tf_op jit(solution)/shard_map/ppermute | solution.py:26
  655.1 2.1 copy-done.7
  (107 shorter events, 20.0 us)
Async XLA Ops:
  7.2 33.2 %copy-start = (bf16[32,8,3584]{2,1,0:T(8,128)(2,1)S(1)}, bf16[32,8,3584]{2,1,0:T(8,128)(2,1)}, u32[]{:S(2)}) copy-start(bf16[32,8,3584]{2,1,0:T(8,128)(2,1)} %param.19) | copy-start | bytes 5505028
  7.2 256.7 %all-gather.6.cloned.1.call-start = ((), (), s32[]{:S(2)}) async-start(), calls=%async_computation.5 | async-start | bytes 2064384 | tf_op jit(solution)/shard_map/all_gather | solution.py:148
  7.9 259.8 %all-gather.4.cloned.1.call-start = ((), (), s32[]{:S(2)}) async-start(), calls=%async_computation.4 | async-start | bytes 2064384 | tf_op jit(solution)/shard_map/all_gather | solution.py:149
  8.7 13.8 %copy-start.13 = (s32[20]{0:T(128)}, s32[20]{0:T(128)S(1)}, u32[]{:S(2)}) copy-start(s32[20]{0:T(128)S(1)} %get-tuple-element.71) | copy-start | bytes 244
  8.7 13.8 %copy-start.15 = (s32[20]{0:T(128)}, s32[20]{0:T(128)S(1)}, u32[]{:S(2)}) copy-start(s32[20]{0:T(128)S(1)} %get-tuple-element.72) | copy-start | bytes 244
  30.7 7.7 %copy-start.2 = (s32[64,1]{0,1:T(1,128)S(1)}, s32[64,1]{0,1:T(1,128)}, u32[]{:S(2)}) copy-start(s32[64,1]{0,1:T(1,128)} %param.20) | copy-start | bytes 772
  30.7 8.3 %copy-start.4 = (s32[64]{0:T(128)S(1)}, s32[64]{0:T(128)}, u32[]{:S(2)}) copy-start(s32[64]{0:T(128)} %param.22) | copy-start | bytes 772
  30.7 203.2 %all-to-all-start = ((bf16[20,64,3584]{2,1,0:T(8,128)(2,1)}), bf16[20,64,3584]{2,1,0:T(8,128)(2,1)}, u32[]{:S(2)}, u32[]{:S(2)}) async-start(bf16[20,64,3584]{2,1,0:T(8,128)(2,1)} %select_select_fusion), calls=%async_computation | async-start | bytes 18350080 | tf_op jit(solution)/shard_map/all_to_all | solution.py:117
  37.0 316.2 %all-gather.8.cloned.1.call-start = ((), (), s32[]{:S(2)}) async-start(), calls=%async_computation.6 | async-start | bytes 14450688 | tf_op jit(solution)/shard_map/all_gather | solution.py:147
  233.9 18.7 %all-to-all-start.2 = ((bf16[16,8,3584]{2,1,0:T(8,128)(2,1)}), bf16[16,8,3584]{2,1,0:T(8,128)(2,1)S(1)}, u32[]{:S(2)}, u32[]{:S(2)}) async-start(bf16[16,8,3584]{2,1,0:T(8,128)(2,1)} %broadcast_select_fusion.2), calls=%async_computation.2 | async-start | bytes 1835008 | tf_op jit(solution)/shard_map/all_to_all | solution.py:125
  252.6 5.9 copy-start.3
  252.6 6.6 copy-start.12
  252.6 6.6 copy-start.5
  252.6 86.6 %all-to-all-start.1 = ((bf16[16,64,3584]{2,1,0:T(8,128)(2,1)}), bf16[16,64,3584]{2,1,0:T(8,128)(2,1)}, u32[]{:S(2)}, u32[]{:S(2)}) async-start(bf16[16,64,3584]{2,1,0:T(8,128)(2,1)} %broadcast_select_fusion), calls=%async_computation.1 | async-start | bytes 14680064 | tf_op jit(solution)/shard_map/all_to_all | solution.py:124
  339.2 3.8 copy-start.8
  343.0 6.1 copy-start.6
  343.0 2.9 copy-start.10
  348.3 1.5 copy-start.9
  477.2 6.5 copy-start.11
  489.3 5.9 copy-start.14
  489.3 5.9 copy-start.16
  489.3 5.9 copy-start.17
  489.3 6.0 copy-start.18
  489.3 48.0 %all-to-all-start.3 = ((bf16[2,512,1792]{2,0,1:T(2,128)(2,1)}), bf16[2,512,1792]{2,0,1:T(2,128)(2,1)}, u32[]{:S(2)}, u32[]{:S(2)}) async-start(bf16[2,512,1792]{2,0,1:T(2,128)(2,1)} %broadcast_select_fusion.1), calls=%async_computation.3 | async-start | bytes 7340032 | tf_op jit(solution)/shard_map/all_to_all | solution.py:168
  550.6 5.4 copy-start.19
  550.6 106.6 %copy-start.1 = (bf16[32,8,3584]{2,1,0:T(8,128)(2,1)S(1)}, bf16[32,8,3584]{2,1,0:T(8,128)(2,1)}, u32[]{:S(2)}) copy-start(bf16[32,8,3584]{2,1,0:T(8,128)(2,1)} %param.19) | copy-start | bytes 5505028
  551.0 51.6 %collective-permute-start = (bf16[5,64,1792]{2,1,0:T(8,128)(2,1)S(1)}, bf16[5,64,1792]{2,1,0:T(8,128)(2,1)S(1)}, u32[]{:S(2)}, u32[]{:S(2)}) collective-permute-start(bf16[5,64,1792]{2,1,0:T(8,128)(2,1)S(1)} %get-tuple-element.61), channel_id=1, source_target_pairs={{0,8},{8,0},{16,24},{24,16},{1,9},{9,1},{17,25},{25,17},{2,10},{10... | collective-permute-start | bytes 3440648 | tf_op jit(solution)/shard_map/ppermute | solution.py:26
  554.4 74.9 %collective-permute-start.1 = (bf16[5,64,1792]{2,1,0:T(8,128)(2,1)S(1)}, bf16[5,64,1792]{2,1,0:T(8,128)(2,1)S(1)}, u32[]{:S(2)}, u32[]{:S(2)}) collective-permute-start(bf16[5,64,1792]{2,1,0:T(8,128)(2,1)S(1)} %get-tuple-element.60), channel_id=1, source_target_pairs={{0,16},{8,24},{16,0},{24,8},{1,17},{9,25},{17,1},{25,9},{2,18},{10... | collective-permute-start | bytes 3440648 | tf_op jit(solution)/shard_map/ppermute | solution.py:26
  554.5 100.5 %collective-permute-start.2 = (bf16[5,64,1792]{2,1,0:T(8,128)(2,1)S(1)}, bf16[5,64,1792]{2,1,0:T(8,128)(2,1)S(1)}, u32[]{:S(2)}, u32[]{:S(2)}) collective-permute-start(bf16[5,64,1792]{2,1,0:T(8,128)(2,1)S(1)} %get-tuple-element.59), channel_id=1, source_target_pairs={{0,24},{8,16},{16,8},{24,0},{1,25},{9,17},{17,9},{25,1},{2,26},{10... | collective-permute-start | bytes 3440648 | tf_op jit(solution)/shard_map/ppermute | solution.py:26
  655.1 2.1 copy-start.7
Sparse Core Ops, SparseCore 0:
  9.9 27.8 all-gather.5
  39.6 26.6 all-gather.3
  68.2 73.0 all-gather.7
